TPU v7x, 256 devices: a whole 4x4x8 slice. The times are simulated.
256 devices in a mesh: stn: 32 (over z, x_lo, core), tm: 8 (over x_hi, y).
Axes of the slice: x: 4 (x_hi: 2, x_lo: 2; x = x_hi * 2 + x_lo), y: 4, z: 8, core: 2. Of those that a mesh axis runs over, the one named last changes fastest.
Arguments:
- voltage: bfloat16 [256, 256, 2, 4096], P('stn', 'tm'), may hold values from -6 to 6
- fir_taps: float32 [16, 4096], replicated, may hold values from -1.5 to 1.5
Outputs:
- visibilities: float32 [2, 256, 32, 2048], P(None, 'stn', None, 'tm')
All inputs are finite; a program needn't handle non-finite values.
Results may differ from a plain program's by a relative error of at most 0.0014.
Values may be sent and summed in bfloat16 or wider, within the bound.
A program may use at most 192 MiB of HBM per device.

v0:
```python
import math
import jax
import jax.numpy as jnp
from jax import lax
from jax.sharding import PartitionSpec as P

NCH = 4096
ROOT = 64
CHANS = 2048
VISITS = 4


def passed_along(block, axis, distance):
    devices = range(lax.axis_size(axis))
    route = [((i - distance) % len(devices), i) for i in devices]
    return lax.ppermute(block, axis, route)


def passed_along_2(shard, axis, by):
    peers = lax.axis_size(axis)
    pairs = [(i, i + by) for i in range(peers) if 0 <= i + by < peers]
    return lax.ppermute(shard, axis, pairs)


def tables(size_a, size_b, modulus, factor):
    left_index = lax.iota(jnp.int32, size_a)[:, None]
    right_index = lax.iota(jnp.int32, size_b)[None, :]
    angles = (left_index * right_index % modulus).astype(jnp.float32) * (2.0 * math.pi / modulus)
    return (jnp.cos(angles) * factor, jnp.sin(angles) * factor)


def real_form(cosine, sine_part):
    from_real = jnp.stack([cosine, -sine_part], axis=1)
    from_imag = jnp.stack([sine_part, cosine], axis=1)
    return jnp.stack([from_real, from_imag], axis=0)


def channelise(voltage, history, fir_taps):
    count_frames = voltage.shape[1]
    signals = voltage.shape[0]
    width_all = 2 * voltage.shape[3]
    extended = jnp.concatenate([history, voltage], 1)
    extended = extended.reshape(signals, extended.shape[1], width_all).astype(jnp.float32)
    kernel = jnp.tile(fir_taps, (1, 2))[:, None, :]
    filtered = lax.conv_general_dilated(
        extended,
        kernel,
        (1,),
        "VALID",
        dimension_numbers=("NHC", "HIO", "NHC"),
        feature_group_count=width_all,
        precision=lax.Precision.HIGHEST,
    )
    grid_form = filtered.reshape(signals, count_frames, 2, ROOT, ROOT)
    cos_one, sin_one = tables(ROOT, ROOT, ROOT, 1.0)
    section_one = jnp.einsum(
        "sfrab,rapk->sfbpk", grid_form, real_form(cos_one, sin_one), precision=lax.Precision.HIGHEST
    )
    cos_turn, sin_turn = tables(ROOT, ROOT, NCH, 1.0)
    real_part = section_one[:, :, :, 0]
    imag_part = section_one[:, :, :, 1]
    turned = jnp.stack(
        [real_part * cos_turn + imag_part * sin_turn, imag_part * cos_turn - real_part * sin_turn],
        3,
    )
    keep_count = CHANS // ROOT
    cos_two, sin_two = tables(ROOT, keep_count, ROOT, 1.0 / math.sqrt(NCH))
    spectrum = jnp.einsum(
        "sfbpk,pbqj->sfqjk", turned, real_form(cos_two, sin_two), precision=lax.Precision.HIGHEST
    )
    return spectrum.reshape(signals, count_frames, 2, CHANS).astype(jnp.bfloat16)


def correlate(own_block, other_block):
    products = jnp.einsum(
        "sfrc,tfqc->rsqtc", own_block, other_block, preferred_element_type=jnp.float32
    )
    real_part = products[0, :, 0] + products[1, :, 1]
    imag_part = products[1, :, 0] - products[0, :, 1]
    return jnp.stack([real_part, imag_part], 0)


def partner_blocks(local_block):
    blocks = [local_block]
    current = local_block
    for visit_index in range(1, VISITS):
        current = passed_along(current, "stn", 1)
        blocks.append(current)
    return blocks


def local(voltage, fir_taps):
    frames_here = voltage.shape[1]
    tail_frames = voltage[:, frames_here - (fir_taps.shape[0] - 1) :]
    history = passed_along_2(tail_frames, "tm", 1)
    spectrum = channelise(voltage, history, fir_taps)
    local_block = lax.all_to_all(spectrum, "tm", split_axis=3, concat_axis=1, tiled=True)
    blocks = partner_blocks(local_block)
    partial_value = jnp.concatenate(
        [correlate(local_block, visiting_block) for visiting_block in blocks], 2
    )
    return partial_value / float(lax.axis_size("tm") * frames_here)


def solution(mesh):
    return jax.shard_map(
        local,
        mesh=mesh,
        in_specs=(P("stn", "tm", None, None), P()),
        out_specs=P(None, "stn", None, "tm"),
        check_vma=False,
    )
```

profile of v0, /device:TPU:99, one launch (start us, length us, event | category | flops | bytes accessed | tf_op | source)
XLA Modules:
  0.0 348.3 jit_solution(5081609641618378158)
XLA Ops:
  0.0 5.3 %slice.57 = bf16[8,15,2,4096]{3,2,1,0:T(2,128)(2,1)} slice(bf16[8,32,2,4096]{3,2,1,0:T(2,128)(2,1)} %param.2), slice={[0:8], [17:32], [0:2], [0:4096]} | slice | bytes 3932160 | tf_op jit(solution)/shard_map/slice | solution.py:94
  5.3 3.3 collective-permute-start
  8.6 1.2 tile.8
  9.8 0.8 tile.9
  10.6 0.1 fusion.47
  10.7 0.1 fusion.46
  10.9 0.1 sine_multiply_fusion
  10.9 0.1 fusion.41
  11.1 0.1 fusion.39
  11.3 39.0 %collective-permute-done = bf16[8,15,2,4096]{3,2,1,0:T(2,128)(2,1)S(1)} collective-permute-done((bf16[8,15,2,4096]{3,2,1,0:T(2,128)(2,1)}, bf16[8,15,2,4096]{3,2,1,0:T(2,128)(2,1)S(1)}, u32[]{:S(2)}, u32[]{:S(2)}) %collective-permute-start) | collective-permute-done | bytes 1966112 | tf_op jit(solution)/shard_map/ppermute | solution.py:22
  50.3 18.0 %pad_maximum_fusion = bf16[8,47,2,4096]{3,2,1,0:T(2,128)(2,1)S(1)} fusion(bf16[8,32,2,4096]{3,2,1,0:T(2,128)(2,1)} %param.2, bf16[8,15,2,4096]{3,2,1,0:T(2,128)(2,1)S(1)} %collective-permute-done), kind=kLoop, calls=%fused_computation.10 | loop fusion | flops 3080192 | bytes 12320768 | tf_op jit(solution)/shard_map/concatenate | solution.py:42
  68.3 7.0 %copy.49 = bf16[8,47,2,4096]{3,0,2,1:T(8,128)(2,1)S(1)} copy(bf16[8,47,2,4096]{3,2,1,0:T(2,128)(2,1)S(1)} %pad_maximum_fusion) | data formatting | bytes 12320768 | tf_op jit(solution)/shard_map/concatenate | solution.py:42
  75.3 10.3 %fusion.50 = f32[8,32,8192]{2,0,1:T(8,128)} fusion(bf16[8,47,8192]{2,0,1:T(8,128)(2,1)S(1)} %bitcast.109, f32[16,1,8192]{2,1,0:T(1,128)S(1)} %tile.9), kind=kOutput, calls=%fused_computation.83 | convolution fusion | flops 402653184 | bytes 15073280 | tf_op jit(solution)/shard_map/conv_general_dilated | solution.py:45
  85.6 14.2 %reshape.351 = f32[8,32,2,64,64]{4,3,2,0,1:T(8,128)} reshape(f32[8,32,8192]{2,0,1:T(8,128)} %fusion.50) | data formatting | bytes 16777216 | tf_op jit(solution)/shard_map/reshape | solution.py:54
  99.8 33.7 %fusion.5 = f32[8,32,64,2,64]{4,2,3,1,0:T(8,128)} fusion(f32[1,64,2,64]{3,1,0,2:T(8,128)S(1)} %get-tuple-element.16, f32[1,64,2,64]{3,1,0,2:T(8,128)S(1)} %get-tuple-element.15, f32[8,32,2,64,64]{4,3,2,0,1:T(8,128)} %reshape.351), kind=kOutput, calls=%fused_computation.6 | convolution fusion | flops 3221241856 | bytes 16842752 | tf_op jit(solution)/shard_map/sfrab,rapk->sfbpk/dot_general | solution.py:56
  133.5 7.2 %multiply_add_fusion = (f32[8,32,64,1,64]{4,2,3,1,0:T(8,128)S(1)}, f32[8,32,64,1,64]{4,2,3,1,0:T(8,128)S(1)}) fusion(f32[8,32,64,2,64]{4,2,3,1,0:T(8,128)} %fusion.5, f32[64,64]{1,0:T(8,128)S(1)} %get-tuple-element.21, f32[64,64]{1,0:T(8,128)S(1)} %get-tuple-element.22), kind=kLoop, calls=%fused_computation.9 | loop fusion | flops 6291456 | bytes 16809984 | tf_op jit(solution)/shard_map/add | solution.py:63
  140.7 12.6 %fusion.8 = bf16[8,32,2,32,64]{4,3,1,0,2:T(8,128)(2,1)} fusion(f32[8,32,64,1,64]{4,2,3,1,0:T(8,128)S(1)} %get-tuple-element.6, f32[8,32,64,1,64]{4,2,3,1,0:T(8,128)S(1)} %get-tuple-element.5, f32[1,64,2,32]{1,3,0,2:T(8,128)S(1)} %get-tuple-element.18, f32[1,64,2,32]{1,3,0,2:T(8,128)S(1)} %get-tuple-element.17), kind=kOutput, calls=%fused_computation.11 | convolution fusion | flops 1613766656 | bytes 10518528 | tf_op jit(solution)/shard_map/sfbpk,pbqj->sfqjk/dot_general | solution.py:68
  153.4 22.4 %copy.84 = bf16[8,32,2,32,64]{1,2,0,4,3:T(2,128)(2,1)} copy(bf16[8,32,2,32,64]{4,3,1,0,2:T(8,128)(2,1)} %fusion.8) | data formatting | bytes 4194304 | tf_op jit(solution)/shard_map/convert_element_type | solution.py:71
  175.7 10.1 %reshape.366 = bf16[8,2,65536]{2,1,0:T(2,128)(2,1)S(1)} reshape(bf16[2048,8,2,32]{3,2,1,0:T(2,128)(2,1)} %bitcast.104) | data formatting | bytes 4194304
  185.9 33.2 %all_to_all.18 = bf16[8,2,65536]{2,1,0:T(2,128)(2,1)} all-to-all(bf16[8,2,65536]{2,1,0:T(2,128)(2,1)S(1)} %reshape.366), channel_id=1, replica_groups=mesh['stn'=32,'tm'=8] {'tm'}, dimensions={0} | all-to-all | bytes 4194304 | tf_op jit(solution)/shard_map/all_to_all | solution.py:97
  219.0 8.7 %reshape.367 = bf16[2048,8,2,32]{3,2,1,0:T(2,128)(2,1)} reshape(bf16[8,2,65536]{2,1,0:T(2,128)(2,1)} %all_to_all.18) | data formatting | bytes 4194304
  227.7 17.8 %copy.86 = bf16[8,32,2,8,256]{4,1,3,2,0:T(8,128)(2,1)S(1)} copy(bf16[8,32,2,8,256]{1,2,0,4,3:T(2,128)(2,1)} %bitcast.105) | data formatting | bytes 4194304 | tf_op jit(solution)/shard_map/all_to_all | solution.py:97
  245.5 3.2 copy.59
  248.7 7.2 %collective-permute-start.1 = (bf16[8,256,2,256]{1,0,2,3:T(8,128)(2,1)}, bf16[8,256,2,256]{1,0,2,3:T(8,128)(2,1)}, u32[]{:S(2)}, u32[]{:S(2)}) collective-permute-start(bf16[8,256,2,256]{1,0,2,3:T(8,128)(2,1)} %copy.59), channel_id=1, source_target_pairs={{248,0},{0,8},{8,16},{16,24},{24,32},{32,40},{40,48},{48,56},{56,6... | collective-permute-start | bytes 6291464 | tf_op jit(solution)/shard_map/ppermute | solution.py:16
  255.9 23.3 %collective-permute-done.1 = bf16[8,256,2,256]{1,0,2,3:T(8,128)(2,1)} collective-permute-done((bf16[8,256,2,256]{1,0,2,3:T(8,128)(2,1)}, bf16[8,256,2,256]{1,0,2,3:T(8,128)(2,1)}, u32[]{:S(2)}, u32[]{:S(2)}) %collective-permute-start.1) | collective-permute-done | bytes 2097184 | tf_op jit(solution)/shard_map/ppermute | solution.py:16
  279.2 4.6 %collective-permute-start.2 = (bf16[8,256,2,256]{1,0,2,3:T(8,128)(2,1)}, bf16[8,256,2,256]{1,0,2,3:T(8,128)(2,1)}, u32[]{:S(2)}, u32[]{:S(2)}) collective-permute-start(bf16[8,256,2,256]{1,0,2,3:T(8,128)(2,1)} %collective-permute-done.1), channel_id=1, source_target_pairs={{248,0},{0,8},{8,16},{16,24},{24,32},{32,40},{40,48},{48,56},{56,6... | collective-permute-start | bytes 6291464 | tf_op jit(solution)/shard_map/ppermute | solution.py:16
  283.8 3.4 copy.75
  287.2 4.6 %copy.74 = bf16[8,256,2,256,1]{1,0,4,2,3:T(8,128)(2,1)} copy(bf16[8,256,2,256,1]{3,1,2,0,4:T(8,128)(2,1)} %bitcast.108) | data formatting | bytes 4194304 | tf_op jit(solution)/shard_map/all_to_all | solution.py:97
  291.8 15.3 %collective-permute-done.2 = bf16[8,256,2,256]{1,0,2,3:T(8,128)(2,1)} collective-permute-done((bf16[8,256,2,256]{1,0,2,3:T(8,128)(2,1)}, bf16[8,256,2,256]{1,0,2,3:T(8,128)(2,1)}, u32[]{:S(2)}, u32[]{:S(2)}) %collective-permute-start.2) | collective-permute-done | bytes 2097184 | tf_op jit(solution)/shard_map/ppermute | solution.py:16
  307.1 4.7 %collective-permute-start.3 = (bf16[8,256,2,256]{1,0,2,3:T(8,128)(2,1)}, bf16[8,256,2,256]{1,0,2,3:T(8,128)(2,1)}, u32[]{:S(2)}, u32[]{:S(2)}) collective-permute-start(bf16[8,256,2,256]{1,0,2,3:T(8,128)(2,1)} %collective-permute-done.2), channel_id=1, source_target_pairs={{248,0},{0,8},{8,16},{16,24},{24,32},{32,40},{40,48},{48,56},{56,6... | collective-permute-start | bytes 6291464 | tf_op jit(solution)/shard_map/ppermute | solution.py:16
  311.8 6.3 %convolution_bitcast_fusion.3 = f32[2,8,2,8,256]{3,1,0,2,4:T(8,128)S(1)} fusion(bf16[8,256,2,256,1]{1,0,4,2,3:T(8,128)(2,1)} %copy.74, bf16[8,256,2,256,1]{1,0,2,4,3:T(8,128)(2,1)S(1)} %copy.75), kind=kOutput, calls=%fused_computation.15 | convolution fusion | flops 33554432 | bytes 4456448 | tf_op jit(solution)/shard_map/sfrc,tfqc->rsqtc/dot_general | solution.py:75
  318.1 1.2 fusion.19
  319.3 1.5 copy.57
  320.9 0.4 copy.58
  321.2 6.3 %convolution_bitcast_fusion.2 = f32[2,8,2,8,256]{3,1,0,2,4:T(8,128)S(1)} fusion(bf16[8,256,2,256,1]{1,0,2,4,3:T(8,128)(2,1)S(1)} %copy.75, bf16[8,256,2,256]{1,0,2,3:T(8,128)(2,1)} %collective-permute-done.1), kind=kOutput, calls=%fused_computation.14 | convolution fusion | flops 33554432 | bytes 4456448 | tf_op jit(solution)/shard_map/sfrc,tfqc->rsqtc/dot_general | solution.py:75
  327.5 1.2 fusion.17
  328.7 1.5 copy.61
  330.2 0.4 copy.62
  330.6 6.3 %convolution_bitcast_fusion.1 = f32[2,8,2,8,256]{3,1,0,2,4:T(8,128)S(1)} fusion(bf16[8,256,2,256,1]{1,0,2,4,3:T(8,128)(2,1)S(1)} %copy.75, bf16[8,256,2,256]{1,0,2,3:T(8,128)(2,1)} %collective-permute-done.2), kind=kOutput, calls=%fused_computation.13 | convolution fusion | flops 33554432 | bytes 4456448 | tf_op jit(solution)/shard_map/sfrc,tfqc->rsqtc/dot_general | solution.py:75
  336.9 1.2 fusion.15
  338.1 1.5 copy.64
  339.6 0.4 copy.65
  340.0 0.0 collective-permute-done.3
  340.0 6.3 %convolution_bitcast_fusion = f32[2,8,2,8,256]{3,1,0,2,4:T(8,128)S(1)} fusion(bf16[8,256,2,256,1]{1,0,2,4,3:T(8,128)(2,1)S(1)} %copy.75, bf16[8,256,2,256]{1,0,2,3:T(8,128)(2,1)} %collective-permute-done.3), kind=kOutput, calls=%fused_computation.12 | convolution fusion | flops 33554432 | bytes 4456448 | tf_op jit(solution)/shard_map/sfrc,tfqc->rsqtc/dot_general | solution.py:75
  346.3 0.2 fusion.13
  346.5 0.3 copy.67
  346.9 0.4 copy.68
  347.2 0.9 maximum_multiply_fusion
  (4 shorter events, 0.0 us)
Async XLA Ops:
  5.3 45.0 %collective-permute-start = (bf16[8,15,2,4096]{3,2,1,0:T(2,128)(2,1)}, bf16[8,15,2,4096]{3,2,1,0:T(2,128)(2,1)S(1)}, u32[]{:S(2)}, u32[]{:S(2)}) collective-permute-start(bf16[8,15,2,4096]{3,2,1,0:T(2,128)(2,1)} %slice.57), channel_id=1, source_target_pairs={{0,1},{1,2},{2,3},{3,4},{4,5},{5,6},{6,7},{8,9},{9,10},{10,11},{11... | collective-permute-start | bytes 5898248 | tf_op jit(solution)/shard_map/ppermute | solution.py:22
  245.5 38.3 %copy-start = (bf16[8,32,2,8,256]{4,1,3,2,0:T(8,128)(2,1)}, bf16[8,32,2,8,256]{4,1,3,2,0:T(8,128)(2,1)S(1)}, u32[]{:S(2)}) copy-start(bf16[8,32,2,8,256]{4,1,3,2,0:T(8,128)(2,1)S(1)} %copy.86) | copy-start | bytes 6291460
  248.7 30.5 %collective-permute-start.1 = (bf16[8,256,2,256]{1,0,2,3:T(8,128)(2,1)}, bf16[8,256,2,256]{1,0,2,3:T(8,128)(2,1)}, u32[]{:S(2)}, u32[]{:S(2)}) collective-permute-start(bf16[8,256,2,256]{1,0,2,3:T(8,128)(2,1)} %copy.59), channel_id=1, source_target_pairs={{248,0},{0,8},{8,16},{16,24},{24,32},{32,40},{40,48},{48,56},{56,6... | collective-permute-start | bytes 6291464 | tf_op jit(solution)/shard_map/ppermute | solution.py:16
  279.2 27.9 %collective-permute-start.2 = (bf16[8,256,2,256]{1,0,2,3:T(8,128)(2,1)}, bf16[8,256,2,256]{1,0,2,3:T(8,128)(2,1)}, u32[]{:S(2)}, u32[]{:S(2)}) collective-permute-start(bf16[8,256,2,256]{1,0,2,3:T(8,128)(2,1)} %collective-permute-done.1), channel_id=1, source_target_pairs={{248,0},{0,8},{8,16},{16,24},{24,32},{32,40},{40,48},{48,56},{56,6... | collective-permute-start | bytes 6291464 | tf_op jit(solution)/shard_map/ppermute | solution.py:16
  307.1 32.9 %collective-permute-start.3 = (bf16[8,256,2,256]{1,0,2,3:T(8,128)(2,1)}, bf16[8,256,2,256]{1,0,2,3:T(8,128)(2,1)}, u32[]{:S(2)}, u32[]{:S(2)}) collective-permute-start(bf16[8,256,2,256]{1,0,2,3:T(8,128)(2,1)} %collective-permute-done.2), channel_id=1, source_target_pairs={{248,0},{0,8},{8,16},{16,24},{24,32},{32,40},{40,48},{48,56},{56,6... | collective-permute-start | bytes 6291464 | tf_op jit(solution)/shard_map/ppermute | solution.py:16
where the time goes:
time: 354 us; the launch traced here: 348 us
  local copies, waits for them, and re-layouts  105 us (30%)
  matrix products  81.8 us (23%)
  waiting for transfers between devices  77.6 us (22%)
  blocking collectives  33.2 us (9%)
  other arithmetic  30.6 us (9%)
  starting transfers between devices  19.9 us (6%)
    ppermute x1, waiting for transfers between devices, passed_along_2(): return lax.ppermute(shard, axis, pairs)  39 us
    ppermute x3, waiting for transfers between devices, passed_along(): return lax.ppermute(block, axis, route)  38.6 us
    dot_general x1, matrix products, channelise(): jnp.einsum('sfrab,rapk->sfbpk', grid_form, real_form(cos_one, sin_one), p...  33.7 us
    all_to_all x1, blocking collectives, local(): lax.all_to_all(spectrum, 'tm', split_axis=3, concat_axis=1, tiled=True)  33.2 us
    all_to_all x4, local copies, waits for them, and re-layouts, local(): lax.all_to_all(spectrum, 'tm', split_axis=3, concat_axis=1, tiled=True)  28.9 us
    dot_general x4, matrix products, correlate(): jnp.einsum('sfrc,tfqc->rsqtc', own_block, other_block, preferred_element_...  25.2 us
    convert_element_type x1, local copies, waits for them, and re-layouts, channelise(): spectrum.reshape(signals, count_frames, 2, CHANS).astype(jnp.bfloat16)  22.4 us
    unnamed x4, local copies, waits for them, and re-layouts  18.8 us
  transfers between devices with their start and end apart: 4, of which 3 were waited for; matrix products, arithmetic and copies ran while one was open for 11% of the time, Pallas kernels for 0%

commit v1 on v0

--- a/solution.py
+++ b/solution.py
@@ -94,7 +94,10 @@
     tail_frames = voltage[:, frames_here - (fir_taps.shape[0] - 1) :]
     history = passed_along_2(tail_frames, "tm", 1)
     spectrum = channelise(voltage, history, fir_taps)
-    local_block = lax.all_to_all(spectrum, "tm", split_axis=3, concat_axis=1, tiled=True)
+    count = lax.axis_size("tm")
+    shards = jnp.stack(jnp.split(spectrum, count, axis=3), axis=0)
+    shards = lax.all_to_all(shards, "tm", split_axis=0, concat_axis=0)
+    local_block = jnp.concatenate(shards, axis=1)
     blocks = partner_blocks(local_block)
     partial_value = jnp.concatenate(
         [correlate(local_block, visiting_block) for visiting_block in blocks], 2

time: 354 us -> 300 us (0.85)
  local copies, waits for them, and re-layouts: 105 us -> 50 us
    all_to_all x4 -> x1, local copies, waits for them, and re-layouts: 28.9 us -> 0.17 us  [local(): shards = lax.all_to_all(shards, 'tm', split_axis=0, concat_axis=0)]
    unnamed x4 -> x11, local copies, waits for them, and re-layouts: 18.8 us -> 0.15 us
    convert_element_type x1, local copies, waits for them, and re-layouts: 22.4 us -> 5.76 us  [channelise(): spectrum.reshape(signals, count_frames, 2, CHANS).astype(jnp.bfloat16)]
    reshape x0 -> x3, local copies, waits for them, and re-layouts: none -> 9.74 us  [local(): local_block = jnp.concatenate(shards, axis=1)]
  transfers between devices with their start and end apart: 4 -> 4, of which waited for: 3 -> 3; matrix products, arithmetic and copies ran while one was open for 11% -> 12% of each run, Pallas kernels for 0% -> 0%
where the time goes in v1:
time: 300 us; the launch traced here: 296 us
  matrix products  81.8 us (27%)
  waiting for transfers between devices  80 us (27%)
  local copies, waits for them, and re-layouts  50 us (17%)
  blocking collectives  33.1 us (11%)
  other arithmetic  30.6 us (10%)
  starting transfers between devices  19.9 us (7%)
    ppermute x3, waiting for transfers between devices, passed_along(): return lax.ppermute(block, axis, route)  40 us
    ppermute x1, waiting for transfers between devices, passed_along_2(): return lax.ppermute(shard, axis, pairs)  39.9 us
    dot_general x1, matrix products, channelise(): jnp.einsum('sfrab,rapk->sfbpk', grid_form, real_form(cos_one, sin_one), p...  33.7 us
    all_to_all x1, blocking collectives, local(): shards = lax.all_to_all(shards, 'tm', split_axis=0, concat_axis=0)  33.1 us
    dot_general x4, matrix products, correlate(): jnp.einsum('sfrc,tfqc->rsqtc', own_block, other_block, preferred_element_...  25.2 us
    concatenate x1, other arithmetic, channelise(): extended = jnp.concatenate([history, voltage], 1)  18 us
    ppermute x3, starting transfers between devices, passed_along(): return lax.ppermute(block, axis, route)  16.5 us
    reshape x1, local copies, waits for them, and re-layouts, channelise(): grid_form = filtered.reshape(signals, count_frames, 2, ROOT, ROOT)  14.2 us
  transfers between devices with their start and end apart: 4, of which 3 were waited for; matrix products, arithmetic and copies ran while one was open for 12% of the time, Pallas kernels for 0%

profile of v1, /device:TPU:99, one launch (start us, length us, event | category | flops | bytes accessed | tf_op | source)
XLA Modules:
  0.0 295.8 jit_solution(11093705099283677198)
XLA Ops:
  0.0 5.3 %slice.57 = bf16[8,15,2,4096]{3,2,1,0:T(2,128)(2,1)} slice(bf16[8,32,2,4096]{3,2,1,0:T(2,128)(2,1)} %param.2), slice={[0:8], [17:32], [0:2], [0:4096]} | slice | bytes 3932160 | tf_op jit(solution)/shard_map/slice | solution.py:94
  5.3 3.3 %collective-permute-start = (bf16[8,15,2,4096]{3,2,1,0:T(2,128)(2,1)}, bf16[8,15,2,4096]{3,2,1,0:T(2,128)(2,1)S(1)}, u32[]{:S(2)}, u32[]{:S(2)}) collective-permute-start(bf16[8,15,2,4096]{3,2,1,0:T(2,128)(2,1)} %slice.57), channel_id=1, source_target_pairs={{0,1},{1,2},{2,3},{3,4},{4,5},{5,6},{6,7},{8,9},{9,10},{10,11},{11... | collective-permute-start | bytes 5898248 | tf_op jit(solution)/shard_map/ppermute | solution.py:22
  8.6 0.3 tile.8
  8.9 0.8 tile.9
  9.7 0.1 fusion.55
  9.8 0.1 fusion.54
  10.0 0.1 sine_multiply_fusion
  10.0 0.1 fusion.49
  10.2 0.1 fusion.47
  10.4 39.9 %collective-permute-done = bf16[8,15,2,4096]{3,2,1,0:T(2,128)(2,1)S(1)} collective-permute-done((bf16[8,15,2,4096]{3,2,1,0:T(2,128)(2,1)}, bf16[8,15,2,4096]{3,2,1,0:T(2,128)(2,1)S(1)}, u32[]{:S(2)}, u32[]{:S(2)}) %collective-permute-start) | collective-permute-done | bytes 1966112 | tf_op jit(solution)/shard_map/ppermute | solution.py:22
  50.3 18.0 %pad_maximum_fusion = bf16[8,47,2,4096]{3,2,1,0:T(2,128)(2,1)S(1)} fusion(bf16[8,32,2,4096]{3,2,1,0:T(2,128)(2,1)} %param.2, bf16[8,15,2,4096]{3,2,1,0:T(2,128)(2,1)S(1)} %collective-permute-done), kind=kLoop, calls=%fused_computation.10 | loop fusion | flops 3080192 | bytes 12320768 | tf_op jit(solution)/shard_map/concatenate | solution.py:42
  68.3 7.0 %copy.39 = bf16[8,47,2,4096]{3,0,2,1:T(8,128)(2,1)S(1)} copy(bf16[8,47,2,4096]{3,2,1,0:T(2,128)(2,1)S(1)} %pad_maximum_fusion) | data formatting | bytes 12320768 | tf_op jit(solution)/shard_map/concatenate | solution.py:42
  75.4 10.3 %fusion.59 = f32[8,32,8192]{2,0,1:T(8,128)} fusion(bf16[8,47,8192]{2,0,1:T(8,128)(2,1)S(1)} %bitcast.138, f32[16,1,8192]{2,1,0:T(1,128)S(1)} %tile.9), kind=kOutput, calls=%fused_computation.100 | convolution fusion | flops 402653184 | bytes 15073280 | tf_op jit(solution)/shard_map/conv_general_dilated | solution.py:45
  85.7 14.2 %reshape.357 = f32[8,32,2,64,64]{4,3,2,0,1:T(8,128)} reshape(f32[8,32,8192]{2,0,1:T(8,128)} %fusion.59) | data formatting | bytes 16777216 | tf_op jit(solution)/shard_map/reshape | solution.py:54
  99.8 33.7 %fusion.5 = f32[8,32,64,2,64]{4,2,3,1,0:T(8,128)} fusion(f32[1,64,2,64]{3,1,0,2:T(8,128)S(1)} %get-tuple-element.24, f32[1,64,2,64]{3,1,0,2:T(8,128)S(1)} %get-tuple-element.23, f32[8,32,2,64,64]{4,3,2,0,1:T(8,128)} %reshape.357), kind=kOutput, calls=%fused_computation.6 | convolution fusion | flops 3221241856 | bytes 16842752 | tf_op jit(solution)/shard_map/sfrab,rapk->sfbpk/dot_general | solution.py:56
  133.6 7.2 %multiply_add_fusion = (f32[8,32,64,1,64]{4,2,3,1,0:T(8,128)S(1)}, f32[8,32,64,1,64]{4,2,3,1,0:T(8,128)S(1)}) fusion(f32[8,32,64,2,64]{4,2,3,1,0:T(8,128)} %fusion.5, f32[64,64]{1,0:T(8,128)S(1)} %get-tuple-element.29, f32[64,64]{1,0:T(8,128)S(1)} %get-tuple-element.30), kind=kLoop, calls=%fused_computation.9 | loop fusion | flops 6291456 | bytes 16809984 | tf_op jit(solution)/shard_map/add | solution.py:63
  140.8 12.6 %fusion.8 = bf16[8,32,2,32,64]{4,3,1,0,2:T(8,128)(2,1)} fusion(f32[8,32,64,1,64]{4,2,3,1,0:T(8,128)S(1)} %get-tuple-element.6, f32[8,32,64,1,64]{4,2,3,1,0:T(8,128)S(1)} %get-tuple-element.5, f32[1,64,2,32]{1,3,0,2:T(8,128)S(1)} %get-tuple-element.26, f32[1,64,2,32]{1,3,0,2:T(8,128)S(1)} %get-tuple-element.25), kind=kOutput, calls=%fused_computation.11 | convolution fusion | flops 1613766656 | bytes 10518528 | tf_op jit(solution)/shard_map/sfbpk,pbqj->sfqjk/dot_general | solution.py:68
  153.4 5.8 %convert_element_type.79 = bf16[8,32,2,2048]{3,1,0,2:T(8,128)(2,1)S(1)} reshape(bf16[8,32,2,32,64]{4,3,1,0,2:T(8,128)(2,1)} %fusion.8) | data formatting | bytes 4194304 | tf_op jit(solution)/shard_map/convert_element_type | solution.py:71
  159.2 0.3 fusion.58
  159.7 33.1 %all_to_all.5 = bf16[8,8,32,2,256]{4,2,3,1,0:T(8,128)(2,1)S(1)} all-to-all(bf16[8,8,32,2,256]{4,2,3,1,0:T(8,128)(2,1)S(1)} %fusion.20), channel_id=1, replica_groups=mesh['stn'=32,'tm'=8] {'tm'}, dimensions={0} | all-to-all | bytes 4194304 | tf_op jit(solution)/shard_map/all_to_all | solution.py:99
  192.8 0.2 copy.50
  192.9 0.0 copy-start
  193.0 3.2 %copy.55 = bf16[8,256,2,256]{1,0,2,3:T(8,128)(2,1)} copy(bf16[8,256,2,256]{3,1,2,0:T(8,128)(2,1)S(1)} %bitcast.135) | data formatting | bytes 4194304 | tf_op jit(solution)/shard_map/reshape | solution.py:100
  196.2 7.2 %collective-permute-start.1 = (bf16[8,256,2,256]{1,0,2,3:T(8,128)(2,1)}, bf16[8,256,2,256]{1,0,2,3:T(8,128)(2,1)}, u32[]{:S(2)}, u32[]{:S(2)}) collective-permute-start(bf16[8,256,2,256]{1,0,2,3:T(8,128)(2,1)} %copy.55), channel_id=1, source_target_pairs={{248,0},{0,8},{8,16},{16,24},{24,32},{32,40},{40,48},{48,56},{56,6... | collective-permute-start | bytes 6291464 | tf_op jit(solution)/shard_map/ppermute | solution.py:16
  203.4 23.3 %collective-permute-done.1 = bf16[8,256,2,256]{1,0,2,3:T(8,128)(2,1)} collective-permute-done((bf16[8,256,2,256]{1,0,2,3:T(8,128)(2,1)}, bf16[8,256,2,256]{1,0,2,3:T(8,128)(2,1)}, u32[]{:S(2)}, u32[]{:S(2)}) %collective-permute-start.1) | collective-permute-done | bytes 2097184 | tf_op jit(solution)/shard_map/ppermute | solution.py:16
  226.7 4.6 %collective-permute-start.2 = (bf16[8,256,2,256]{1,0,2,3:T(8,128)(2,1)}, bf16[8,256,2,256]{1,0,2,3:T(8,128)(2,1)}, u32[]{:S(2)}, u32[]{:S(2)}) collective-permute-start(bf16[8,256,2,256]{1,0,2,3:T(8,128)(2,1)} %collective-permute-done.1), channel_id=1, source_target_pairs={{248,0},{0,8},{8,16},{16,24},{24,32},{32,40},{40,48},{48,56},{56,6... | collective-permute-start | bytes 6291464 | tf_op jit(solution)/shard_map/ppermute | solution.py:16
  231.3 3.2 %copy.70 = bf16[8,256,2,256,1]{1,0,4,2,3:T(8,128)(2,1)} copy(bf16[8,256,2,256,1]{3,1,2,0,4:T(8,128)(2,1)S(1)} %bitcast.136) | data formatting | bytes 4194304 | tf_op jit(solution)/shard_map/reshape | solution.py:100
  234.4 3.4 %copy.71 = bf16[8,256,2,256,1]{1,0,2,4,3:T(8,128)(2,1)S(1)} copy(bf16[8,256,2,256,1]{3,1,2,0,4:T(8,128)(2,1)} %bitcast.137) | data formatting | bytes 4194304 | tf_op jit(solution)/shard_map/reshape | solution.py:100
  237.8 16.7 %collective-permute-done.2 = bf16[8,256,2,256]{1,0,2,3:T(8,128)(2,1)} collective-permute-done((bf16[8,256,2,256]{1,0,2,3:T(8,128)(2,1)}, bf16[8,256,2,256]{1,0,2,3:T(8,128)(2,1)}, u32[]{:S(2)}, u32[]{:S(2)}) %collective-permute-start.2) | collective-permute-done | bytes 2097184 | tf_op jit(solution)/shard_map/ppermute | solution.py:16
  254.6 4.7 %collective-permute-start.3 = (bf16[8,256,2,256]{1,0,2,3:T(8,128)(2,1)}, bf16[8,256,2,256]{1,0,2,3:T(8,128)(2,1)}, u32[]{:S(2)}, u32[]{:S(2)}) collective-permute-start(bf16[8,256,2,256]{1,0,2,3:T(8,128)(2,1)} %collective-permute-done.2), channel_id=1, source_target_pairs={{248,0},{0,8},{8,16},{16,24},{24,32},{32,40},{40,48},{48,56},{56,6... | collective-permute-start | bytes 6291464 | tf_op jit(solution)/shard_map/ppermute | solution.py:16
  259.3 6.3 %convolution_bitcast_fusion.3 = f32[2,8,2,8,256]{3,1,0,2,4:T(8,128)S(1)} fusion(bf16[8,256,2,256,1]{1,0,4,2,3:T(8,128)(2,1)} %copy.70, bf16[8,256,2,256,1]{1,0,2,4,3:T(8,128)(2,1)S(1)} %copy.71), kind=kOutput, calls=%fused_computation.15 | convolution fusion | flops 33554432 | bytes 4456448 | tf_op jit(solution)/shard_map/sfrc,tfqc->rsqtc/dot_general | solution.py:75
  265.6 1.2 fusion.19
  266.8 1.5 copy.53
  268.3 0.4 copy.54
  268.7 6.3 %convolution_bitcast_fusion.2 = f32[2,8,2,8,256]{3,1,0,2,4:T(8,128)S(1)} fusion(bf16[8,256,2,256,1]{1,0,2,4,3:T(8,128)(2,1)S(1)} %copy.71, bf16[8,256,2,256]{1,0,2,3:T(8,128)(2,1)} %collective-permute-done.1), kind=kOutput, calls=%fused_computation.14 | convolution fusion | flops 33554432 | bytes 4456448 | tf_op jit(solution)/shard_map/sfrc,tfqc->rsqtc/dot_general | solution.py:75
  275.0 1.2 fusion.17
  276.2 1.5 copy.57
  277.7 0.4 copy.58
  278.1 6.3 %convolution_bitcast_fusion.1 = f32[2,8,2,8,256]{3,1,0,2,4:T(8,128)S(1)} fusion(bf16[8,256,2,256,1]{1,0,2,4,3:T(8,128)(2,1)S(1)} %copy.71, bf16[8,256,2,256]{1,0,2,3:T(8,128)(2,1)} %collective-permute-done.2), kind=kOutput, calls=%fused_computation.13 | convolution fusion | flops 33554432 | bytes 4456448 | tf_op jit(solution)/shard_map/sfrc,tfqc->rsqtc/dot_general | solution.py:75
  284.4 1.2 fusion.15
  285.6 1.5 copy.60
  287.1 0.4 copy.61
  287.5 0.0 collective-permute-done.3
  287.5 6.3 %convolution_bitcast_fusion = f32[2,8,2,8,256]{3,1,0,2,4:T(8,128)S(1)} fusion(bf16[8,256,2,256,1]{1,0,2,4,3:T(8,128)(2,1)S(1)} %copy.71, bf16[8,256,2,256]{1,0,2,3:T(8,128)(2,1)} %collective-permute-done.3), kind=kOutput, calls=%fused_computation.12 | convolution fusion | flops 33554432 | bytes 4456448 | tf_op jit(solution)/shard_map/sfrc,tfqc->rsqtc/dot_general | solution.py:75
  293.8 0.2 fusion.13
  294.0 0.3 copy.63
  294.3 0.4 copy.64
  294.7 0.9 maximum_multiply_fusion
  (13 shorter events, 0.2 us)
Async XLA Ops:
  0.0 8.6 %copy-start.1 = (f32[16,4096]{1,0:T(8,128)S(1)}, f32[16,4096]{1,0:T(8,128)}, u32[]{:S(2)}) copy-start(f32[16,4096]{1,0:T(8,128)} %param.3) | copy-start | bytes 786436
  5.3 45.0 %collective-permute-start = (bf16[8,15,2,4096]{3,2,1,0:T(2,128)(2,1)}, bf16[8,15,2,4096]{3,2,1,0:T(2,128)(2,1)S(1)}, u32[]{:S(2)}, u32[]{:S(2)}) collective-permute-start(bf16[8,15,2,4096]{3,2,1,0:T(2,128)(2,1)} %slice.57), channel_id=1, source_target_pairs={{0,1},{1,2},{2,3},{3,4},{4,5},{5,6},{6,7},{8,9},{9,10},{10,11},{11... | collective-permute-start | bytes 5898248 | tf_op jit(solution)/shard_map/ppermute | solution.py:22
  192.9 38.3 %copy-start = (bf16[8,8,32,2,256]{4,2,0,3,1:T(8,128)(2,1)}, bf16[8,8,32,2,256]{4,2,0,3,1:T(8,128)(2,1)S(1)}, u32[]{:S(2)}) copy-start(bf16[8,8,32,2,256]{4,2,0,3,1:T(8,128)(2,1)S(1)} %copy.50) | copy-start | bytes 6291460
  196.2 30.5 %collective-permute-start.1 = (bf16[8,256,2,256]{1,0,2,3:T(8,128)(2,1)}, bf16[8,256,2,256]{1,0,2,3:T(8,128)(2,1)}, u32[]{:S(2)}, u32[]{:S(2)}) collective-permute-start(bf16[8,256,2,256]{1,0,2,3:T(8,128)(2,1)} %copy.55), channel_id=1, source_target_pairs={{248,0},{0,8},{8,16},{16,24},{24,32},{32,40},{40,48},{48,56},{56,6... | collective-permute-start | bytes 6291464 | tf_op jit(solution)/shard_map/ppermute | solution.py:16
  226.7 27.9 %collective-permute-start.2 = (bf16[8,256,2,256]{1,0,2,3:T(8,128)(2,1)}, bf16[8,256,2,256]{1,0,2,3:T(8,128)(2,1)}, u32[]{:S(2)}, u32[]{:S(2)}) collective-permute-start(bf16[8,256,2,256]{1,0,2,3:T(8,128)(2,1)} %collective-permute-done.1), channel_id=1, source_target_pairs={{248,0},{0,8},{8,16},{16,24},{24,32},{32,40},{40,48},{48,56},{56,6... | collective-permute-start | bytes 6291464 | tf_op jit(solution)/shard_map/ppermute | solution.py:16
  254.6 32.9 %collective-permute-start.3 = (bf16[8,256,2,256]{1,0,2,3:T(8,128)(2,1)}, bf16[8,256,2,256]{1,0,2,3:T(8,128)(2,1)}, u32[]{:S(2)}, u32[]{:S(2)}) collective-permute-start(bf16[8,256,2,256]{1,0,2,3:T(8,128)(2,1)} %collective-permute-done.2), channel_id=1, source_target_pairs={{248,0},{0,8},{8,16},{16,24},{24,32},{32,40},{40,48},{48,56},{56,6... | collective-permute-start | bytes 6291464 | tf_op jit(solution)/shard_map/ppermute | solution.py:16
